TPU v7x, 32 devices: a whole 2x2x4 slice. The times are simulated.
32 devices in a mesh: col: 4 (over y, core), fac: 8 (over z, x).
Axes of the slice: x: 2, y: 2, z: 4, core: 2. Of those that a mesh axis runs over, the one named last changes fastest.
Arguments:
- facets: bfloat16 [2, 4096, 4096], P(None, 'col', 'fac'), may hold values from -6 to 6
- row_taper: float32 [4096], P('col'), may hold values from 0.5 to 1.5
- column_taper: float32 [4096], replicated, may hold values from 0.5 to 1.5
- column_place: int32 [1], replicated, may hold values from 0 to 511
- row_offset: int32 [4], replicated, may hold values from 0 to 4095
- column_offset: int32 [8], replicated, may hold values from 0 to 4095
- slot_subgrid: int32 [4, 8], replicated, may hold values from 0 to 7, each once within a row
Outputs:
- subgrids: float32 [4, 8, 2, 512, 128], P('col', 'fac')
All inputs are finite; a program needn't handle non-finite values.
Results may differ from a plain program's by a relative error of at most 0.0052.
Values may be sent and summed in bfloat16 or wider, within the bound.
A program may use at most 64 MiB of HBM per device.

v0:
```python
import math

import jax
import jax.numpy as jnp
from jax import lax
from jax.sharding import PartitionSpec as P

FACET = 4096
STRIP = 128
SUBGRID = 512


def phase_table(starts, positions):
    offsets = jnp.arange(STRIP, dtype=jnp.int32)
    frequency = (starts[:, None] + offsets[None, :]) % FACET
    phases = frequency[:, :, None] * positions[None, None, :] % FACET
    angles = phases.astype(jnp.float32) * (2.0 * math.pi / FACET)
    norm_scale = 1.0 / math.sqrt(FACET)
    return jnp.stack([jnp.cos(angles) * norm_scale, -jnp.sin(angles) * norm_scale]).astype(
        jnp.bfloat16
    )


def complex_rows(table_rows, real_part, imag_part):
    row_total = table_rows.shape[1]
    stacked = table_rows.reshape(2 * row_total, table_rows.shape[2])
    first_product = jnp.dot(stacked, real_part, preferred_element_type=jnp.float32)
    second = jnp.dot(stacked, imag_part, preferred_element_type=jnp.float32)
    return (
        first_product[:row_total] - second[row_total:],
        second[:row_total] + first_product[row_total:],
    )


def complex_cols(table_rows, real_part, imag_part):
    row_total = table_rows.shape[1]
    stacked = table_rows.reshape(2 * row_total, table_rows.shape[2])
    contract_dims = (((1,), (1,)), ((), ()))
    first_product = lax.dot_general(
        stacked, real_part, contract_dims, preferred_element_type=jnp.float32
    )
    second = lax.dot_general(stacked, imag_part, contract_dims, preferred_element_type=jnp.float32)
    return (
        first_product[:row_total] - second[row_total:],
        second[:row_total] + first_product[row_total:],
    )


def on_device(
    facets, row_taper, column_taper, column_place, row_offset, column_offset, slot_subgrid
):
    slot_total = lax.axis_size("fac")
    column_group = lax.axis_index("col")
    facet_index = lax.axis_index("fac")
    row_total = facets.shape[1]
    block_width = facets.shape[2]
    facet_parts = FACET // block_width
    first_row = column_group * row_total
    first_col = facet_index % facet_parts * block_width
    column_gain = lax.dynamic_slice_in_dim(column_taper, first_col, block_width, 0)
    prepared = (
        facets.astype(jnp.float32) * row_taper[None, :, None] * column_gain[None, None, :]
    ).astype(jnp.bfloat16)
    offsets = jnp.arange(STRIP, dtype=jnp.int32)
    row_index = first_row + jnp.arange(row_total, dtype=jnp.int32)
    encode = phase_table(row_offset, row_index).reshape(2, row_offset.shape[0] * STRIP, row_total)
    real_out, imag_out = complex_rows(encode, prepared[0], prepared[1])
    strip_sum = lax.psum_scatter(
        jnp.concatenate([real_out, imag_out], axis=1), "col", scatter_dimension=0, tiled=True
    )
    strip = strip_sum.astype(jnp.bfloat16)
    strip_real = strip[:, :block_width]
    strip_imag = strip[:, block_width:]
    owned_slots = lax.dynamic_index_in_dim(slot_subgrid, column_group, 0, keepdims=False)
    starts = jnp.take(column_offset, owned_slots)
    column_index = first_col + jnp.arange(block_width, dtype=jnp.int32)
    decode = phase_table(starts, column_index).reshape(2, slot_total * STRIP, block_width)
    real_out, imag_out = complex_cols(decode, strip_real, strip_imag)
    contribution = jnp.stack(
        [real_out.reshape(slot_total, STRIP, STRIP), imag_out.reshape(slot_total, STRIP, STRIP)]
    )
    received = lax.all_to_all(contribution, "fac", split_axis=1, concat_axis=1, tiled=True)
    sources = jnp.arange(slot_total, dtype=jnp.int32)
    targets = (
        (jnp.take(column_place, sources // facet_parts)[:, None] + offsets[None, :]) % SUBGRID
    ).reshape(-1)
    merged = received.reshape(2, slot_total * STRIP, STRIP)
    subgrid = jnp.zeros((2, SUBGRID, STRIP), jnp.float32).at[:, targets, :].add(merged)
    return subgrid.reshape(1, 1, 2, SUBGRID, STRIP)


def solution(mesh):
    in_specs = (P(None, "col", "fac"), P("col"), P(), P(), P(), P(), P())
    out_specs = P("col", "fac", None, None, None)
    return jax.shard_map(
        on_device, mesh=mesh, in_specs=in_specs, out_specs=out_specs, check_vma=False
    )
```

profile of v0, /device:TPU:0, one launch (start us, length us, event | category | flops | bytes accessed | tf_op | source)
XLA Modules:
  0.0 134.3 jit_solution(8893976778812239895)
XLA Ops:
  6.5 0.0 copy-start
  6.5 0.0 reduce-scatter.2.cloned.1.call-start
  6.5 0.7 add_select_fusion.3
  7.3 0.8 dynamic_slice.8
  8.0 9.1 %multiply_convert_fusion.2 = (bf16[1,4,128,1024]{3,2,1,0:T(8,128)(2,1)S(1)}, bf16[1,4,128,1024]{3,2,1,0:T(8,128)(2,1)S(1)}) fusion(s32[1024]{0:T(1024)S(1)} %iota_add_fusion, s32[4,128]{1,0:T(4,128)S(1)} %add_select_fusion.3), kind=kLoop, calls=%fused_computation.23 | loop fusion | flops 9961472 | bytes 2103296 | tf_op jit(solution)/shard_map/convert
  17.1 0.0 copy-start.1
  17.1 0.0 copy-start.2
  17.1 0.2 pad_maximum_fusion.1
  17.3 1.4 %copy-done.1 = bf16[2,1024,512]{2,1,0:T(8,128)(2,1)S(1)} copy-done((bf16[2,1024,512]{2,1,0:T(8,128)(2,1)S(1)}, bf16[2,1024,512]{2,1,0:T(8,128)(2,1)}, u32[]{:S(2)}) %copy-start.1) | copy-done | bytes 2097176
  18.7 0.0 copy-done.2
  18.7 0.5 multiply_convert_fusion
  19.3 1.3 fusion.6
  20.6 1.3 fusion.7
  21.9 0.5 slice_subtract_fusion
  22.4 1.5 %pad_maximum_fusion.2 = f32[512,1024]{0,1:T(8,128)} fusion(f32[512,512]{0,1:T(8,128)S(1)} %get-tuple-element.6, f32[512,512]{0,1:T(8,128)S(1)} %get-tuple-element.5), kind=kLoop, calls=%fused_computation.21 | loop fusion | flops 524288 | bytes 4194304 | tf_op jit(solution)/shard_map/concatenate | solution.py:69
  23.9 0.0 copy-start.3
  23.9 0.0 reduce-scatter.2.cloned.1.call-update
  23.9 0.7 copy-done.3
  24.6 0.0 copy-done
  24.6 0.6 gather_fusion
  25.3 0.1 add_select_fusion.2
  25.3 9.2 %multiply_convert_fusion.4 = (bf16[1,8,128,512]{3,2,1,0:T(8,128)(2,1)S(1)}, bf16[1,8,128,512]{3,2,1,0:T(8,128)(2,1)S(1)}) fusion(s32[512]{0:T(512)S(1)} %iota_add_fusion.2, s32[8,128]{1,0:T(8,128)S(1)} %add_select_fusion.2), kind=kLoop, calls=%fused_computation.25 | loop fusion | flops 9961472 | bytes 2103296 | tf_op jit(solution)/shard_map/convert.2
  34.5 0.2 pad_maximum_fusion
  34.7 23.3 %reduce-scatter.2.cloned.1.call-done = f32[128,1024]{0,1:T(8,128)} async-done(((f32[512,1024]{0,1:T(8,128)}), f32[128,1024]{0,1:T(8,128)}) %reduce-scatter.2.cloned.1.call-update) | async-done | bytes 524304 | tf_op jit(solution)/shard_map/reduce_scatter | solution.py:68
  58.0 1.1 convert_element_type.63
  59.1 0.7 fusion.10
  59.8 0.7 fusion.8
  60.5 0.1 slice_subtract_fusion.1
  60.6 1.0 pad_maximum_fusion.3
  61.6 5.5 %all-to-all-start = ((f32[2,8,128,128]{3,2,0,1:T(8,128)}), f32[2,8,128,128]{3,2,0,1:T(8,128)S(1)}, u32[]{:S(2)}, u32[]{:S(2)}) async-start(f32[2,8,128,128]{3,2,0,1:T(8,128)} %pad_maximum_fusion.3), calls=%async_computation.1 | async-start | bytes 2097152 | tf_op jit(solution)/shard_map/all_to_all | solution.py:82
  67.8 0.1 iota_add_fusion.1
  67.9 24.9 %all-to-all-done = f32[2,8,128,128]{3,2,0,1:T(8,128)S(1)} async-done(((f32[2,8,128,128]{3,2,0,1:T(8,128)}), f32[2,8,128,128]{3,2,0,1:T(8,128)S(1)}, u32[]{:S(2)}, u32[]{:S(2)}) %all-to-all-start) | async-done | bytes 1048608 | tf_op jit(solution)/shard_map/all_to_all | solution.py:82
  92.8 0.1 copy.17
  92.9 0.8 copy.18
  93.7 0.1 broadcast_in_dim.4
  93.8 32.8 %scatter_fusion = f32[2,512,128]{2,0,1:T(2,128)S(1)} fusion(f32[2,512,128]{2,0,1:T(2,128)S(1)} %broadcast_in_dim.4, s32[1024]{0:T(1024)S(1)} %bitcast.40, f32[1024,2,128]{2,1,0:T(2,128)S(1)} %copy.18), kind=kCustom, calls=%fused_computation.1 | custom fusion | flops 262144 | bytes 3149824 | tf_op jit(solution)/shard_map/scatter-add | solution.py:88
  126.6 0.8 copy.19
  (7 shorter events, 0.1 us)
Async XLA Ops:
  6.5 18.1 %copy-start = (s32[8]{0:T(128)S(1)}, s32[8]{0:T(128)}, u32[]{:S(2)}) copy-start(s32[8]{0:T(128)} %param.12) | copy-start | bytes 100
  6.5 51.5 %reduce-scatter.2.cloned.1.call-start = ((), (), s32[]{:S(2)}) async-start(), calls=%async_computation.2 | async-start | bytes 2621440 | tf_op jit(solution)/shard_map/reduce_scatter | solution.py:68
  17.1 1.6 %copy-start.1 = (bf16[2,1024,512]{2,1,0:T(8,128)(2,1)S(1)}, bf16[2,1024,512]{2,1,0:T(8,128)(2,1)}, u32[]{:S(2)}) copy-start(bf16[2,1024,512]{2,1,0:T(8,128)(2,1)} %param.7) | copy-start | bytes 6291460
  17.1 1.6 %copy-start.2 = (f32[1024]{0:T(1024)S(1)}, f32[1024]{0:T(1024)}, u32[]{:S(2)}) copy-start(f32[1024]{0:T(1024)} %param.8) | copy-start | bytes 12292
  23.9 0.7 copy-start.3
  61.6 31.2 %all-to-all-start = ((f32[2,8,128,128]{3,2,0,1:T(8,128)}), f32[2,8,128,128]{3,2,0,1:T(8,128)S(1)}, u32[]{:S(2)}, u32[]{:S(2)}) async-start(f32[2,8,128,128]{3,2,0,1:T(8,128)} %pad_maximum_fusion.3), calls=%async_computation.1 | async-start | bytes 2097152 | tf_op jit(solution)/shard_map/all_to_all | solution.py:82
Sparse Core Ops, SparseCore 0:
  24.0 33.9 reduce-scatter.1
where the time goes:
time: 135 us; the launch traced here: 134 us
  other arithmetic  57.1 us (42%)
  waiting for transfers between devices  48.2 us (36%)
  between operations  14.2 us (11%)
  starting transfers between devices  5.49 us (4%)
  local copies, waits for them, and re-layouts  5.29 us (4%)
  matrix products  4.02 us (3%)
    scatter-add x1, other arithmetic, on_device(): jnp.zeros((2, SUBGRID, STRIP), jnp.float32).at[:, targets, :].add(merged)  32.8 us
    all_to_all x1, waiting for transfers between devices, on_device(): lax.all_to_all(contribution, 'fac', split_axis=1, concat_axis=1, tiled=True)  24.9 us
    reduce_scatter x1, waiting for transfers between devices, on_device(): lax.psum_scatter(jnp.concatenate([real_out, imag_out], axis=1), 'col', sc...  23.3 us
    another operation x2, other arithmetic  18.2 us
    all_to_all x1, starting transfers between devices, on_device(): lax.all_to_all(contribution, 'fac', split_axis=1, concat_axis=1, tiled=True)  5.49 us
  transfers between devices with their start and end apart: 2, of which 2 were waited for; matrix products, arithmetic and copies ran while one was open for 8% of the time, Pallas kernels for 0%

commit v1 on v0

v1 whole, which is shorter than its diff:
```python
import functools
import math

import jax
import jax.numpy as jnp
from jax import lax
from jax.experimental import pallas as pl
from jax.experimental.pallas import tpu as pltpu
from jax.sharding import PartitionSpec as P

FACET = 4096
STRIP = 128
SUBGRID = 512
FINE = 16
CHUNKS = 4
CHUNK = STRIP // CHUNKS
MESH = pl.DeviceIdType.MESH


def unit_phase(phases):
    quarter = FACET // 4
    shifted = phases + quarter // 2
    angle = ((shifted & (quarter - 1)) - quarter // 2).astype(jnp.float32) * (2.0 * math.pi / FACET)
    turn = lax.shift_right_logical(shifted & (FACET - 1), quarter.bit_length() - 1)
    sq = angle * angle
    cosine = 1.0 + sq * (-1 / 2 + sq * (1 / 24 + sq * (-1 / 720 + sq * (1 / 40320))))
    sine = angle * (1.0 + sq * (-1 / 6 + sq * (1 / 120 + sq * (-1 / 5040 + sq * (1 / 362880)))))
    odd = (turn & 1) == 1
    first = jnp.where(odd, sine, cosine)
    second = jnp.where(odd, cosine, sine)
    real = jnp.where(((turn + 1) & 2) == 2, -first, first)
    imag = jnp.where((turn & 2) == 2, second, -second)
    return real, imag


def iota(shape, dim):
    return lax.broadcasted_iota(jnp.int32, shape, dim)


def kernel(
    cols, facs,
    row_offset, column_offset, slot_subgrid, column_place, row_taper, column_taper, facets,
    out,
    held, coarse_r, coarse_i, fine_r, fine_i, encode, decode_r, decode_i,
    pair_out, pair_in, far_part, far_out, far_in, own_part, strip, strip_in,
    half, mine, slots_out, slots_in,
    held_sem, pair_send, pair_recv, far_send, far_recv, strip_send, strip_recv, slot_send, slot_recv,
):
    col = lax.axis_index("col")
    fac = lax.axis_index("fac")
    col_hi, core = col // 2, col % 2
    fac_hi, fac_lo = fac // 2, fac % 2
    highs, zs = cols // 2, facs // 2
    rows, width = facets.shape[1], facets.shape[2]

    pair_id = (col_hi * 2 + 1 - core, fac)
    far_ids = [((col_hi + d) % highs * 2 + core, fac) for d in range(1, highs)]
    strip_id = (col, fac_hi * 2 + 1 - fac_lo)
    slot_ids = [(col, (fac_hi + d) % zs * 2 + fac_lo) for d in range(1, zs)]
    peers = [pair_id, *far_ids, strip_id, *slot_ids]
    barrier = pltpu.get_barrier_semaphore()
    for peer in peers:
        pl.semaphore_signal(barrier, inc=1, device_id=peer, device_id_type=MESH)
    loads = [pltpu.make_async_copy(facets.at[p], held.at[p], held_sem.at[p]) for p in range(2)]
    for load in loads:
        load.start()

    steps = STRIP // FINE
    position = col * rows + iota((1, rows), 1)
    fine_r[...], fine_i[...] = unit_phase(iota((FINE, rows), 0) * position)
    gain = row_taper[...] * (1.0 / math.sqrt(FACET))

    def encode_group(index, group):
        first = (row_offset[group] + FINE * iota((steps, rows), 0)) & (FACET - 1)
        real, imag = unit_phase(first * position)
        coarse_r[...] = real * gain
        coarse_i[...] = imag * gain

        def row(i, carry):
            ar, ai = coarse_r[pl.ds(i, 1), :], coarse_i[pl.ds(i, 1), :]
            br, bi = fine_r[...], fine_i[...]
            at = pl.multiple_of(i * FINE, FINE)
            encode[index, pl.ds(at, FINE), :] = (ar * br - ai * bi).astype(jnp.bfloat16)
            encode[index, pl.ds(at + STRIP, FINE), :] = (ar * bi + ai * br).astype(jnp.bfloat16)
            return carry

        lax.fori_loop(0, steps, row, 0)

    def product(index):
        table = encode[index]
        by_real = jnp.dot(table, held[0], preferred_element_type=jnp.float32)
        by_imag = jnp.dot(table, held[1], preferred_element_type=jnp.float32)
        return by_real[:STRIP] - by_imag[STRIP:], by_imag[:STRIP] + by_real[STRIP:]

    def chunked(target, real, imag):
        for j in range(CHUNKS):
            span = slice(j * CHUNK, (j + 1) * CHUNK)
            target[j, :CHUNK] = real[span].astype(target.dtype)
            target[j, CHUNK:] = imag[span].astype(target.dtype)

    def pair_copy(d, j):
        return pltpu.make_async_remote_copy(
            src_ref=pair_out.at[d, j], dst_ref=pair_in.at[d, j], send_sem=pair_send.at[d, j],
            recv_sem=pair_recv.at[d, j], device_id=pair_id, device_id_type=MESH)

    def far_copy(d, j):
        return pltpu.make_async_remote_copy(
            src_ref=far_out.at[d - 1, j], dst_ref=far_in.at[d - 1, j], send_sem=far_send.at[d - 1, j],
            recv_sem=far_recv.at[d - 1, j], device_id=far_ids[d - 1], device_id_type=MESH)

    def strip_copy(j):
        return pltpu.make_async_remote_copy(
            src_ref=strip.at[j], dst_ref=strip_in.at[j], send_sem=strip_send.at[j],
            recv_sem=strip_recv.at[j], device_id=strip_id, device_id_type=MESH)

    def slot_copy(d, j):
        return pltpu.make_async_remote_copy(
            src_ref=slots_out.at[d - 1, j], dst_ref=slots_in.at[d - 1, j], send_sem=slot_send.at[d - 1, j],
            recv_sem=slot_recv.at[d - 1, j], device_id=slot_ids[d - 1], device_id_type=MESH)

    order = [*range(1, highs), 0]
    for d in order:
        high = (col_hi + d) % highs * 2
        encode_group(2 * d, high + 1 - core)
        encode_group(2 * d + 1, high + core)

    for load in loads:
        load.wait()
    pl.semaphore_wait(barrier, len(peers))

    def to_pair(d):
        chunked(pair_out.at[d], *product(2 * d))
        for j in range(CHUNKS):
            pair_copy(d, j).start()

    for d in range(1, highs):
        to_pair(d)
        chunked(far_part.at[d - 1], *product(2 * d + 1))
    to_pair(0)
    for d in range(1, highs):
        for j in range(CHUNKS):
            pair_copy(d, j).wait_recv()
            far_out[d - 1, j] = (far_part[d - 1, j] + pair_in[d, j].astype(jnp.float32)).astype(jnp.bfloat16)
            far_copy(d, j).start()
    chunked(own_part, *product(1))

    lanes = zs * STRIP
    coarse_n = width // FINE
    starts = []
    for d in range(zs):
        start = column_offset[slot_subgrid[col, (fac_hi + d) % zs * 2 + fac_lo]]
        starts.append((start + iota((1, STRIP), 1)) & (FACET - 1))
    frequency = jnp.concatenate(starts, axis=1)
    fine_real, fine_imag = unit_phase(iota((FINE, lanes), 0) * frequency)
    fine_real, fine_imag = fine_real * (1.0 / math.sqrt(FACET)), fine_imag * (1.0 / math.sqrt(FACET))
    for part, block in enumerate((fac, fac_hi * 2 + 1 - fac_lo)):
        base = part * width

        def row(i, carry, base=base, block=block):
            ar, ai = unit_phase((block * width + i * FINE) * frequency)
            at = pl.multiple_of(base + i * FINE, FINE)
            decode_r[pl.ds(at, FINE), :] = (ar * fine_real - ai * fine_imag).astype(jnp.bfloat16)
            decode_i[pl.ds(at, FINE), :] = (ar * fine_imag + ai * fine_real).astype(jnp.bfloat16)
            return carry

        lax.fori_loop(0, coarse_n, row, 0)

    column_gain = column_taper[:, pl.ds(pl.multiple_of(fac * width, width), width)]

    def decoded(block, part):
        span = slice(part * width, (part + 1) * width)
        by_real = jnp.dot(block, decode_r[span], preferred_element_type=jnp.float32)
        by_imag = jnp.dot(block, decode_i[span], preferred_element_type=jnp.float32)
        return jnp.concatenate(
            [by_real[:CHUNK] - by_imag[CHUNK:], by_imag[:CHUNK] + by_real[CHUNK:]], axis=0)

    def finish(j):
        strip_copy(j).wait_recv()
        total = half[j] + decoded(strip_in[j], 1)
        mine[j] = total[:, :STRIP]
        for d in range(1, zs):
            slots_out[d - 1, j] = total[:, d * STRIP:(d + 1) * STRIP].astype(jnp.bfloat16)
            slot_copy(d, j).start()

    for j in range(CHUNKS):
        pair_copy(0, j).wait_recv()
        total = own_part[j] + pair_in[0, j].astype(jnp.float32)
        for d in range(1, highs):
            far_copy(d, j).wait_recv()
            total = total + far_in[d - 1, j].astype(jnp.float32)
        strip[j] = (total * column_gain).astype(jnp.bfloat16)
        strip_copy(j).start()
        half[j] = decoded(strip[j], 0)
        if j:
            finish(j - 1)
    finish(CHUNKS - 1)

    place = (iota((SUBGRID, STRIP), 0) - column_place[0]) & (SUBGRID - 1)
    chosen = (place == iota((SUBGRID, STRIP), 1)).astype(jnp.bfloat16)
    sums = []
    for j in range(CHUNKS):
        total = mine[j]
        for d in range(1, zs):
            slot_copy(d, j).wait_recv()
            total = total + slots_in[d - 1, j].astype(jnp.float32)
        sums.append(total)
    for part in range(2):
        value = jnp.concatenate([s[part * CHUNK:(part + 1) * CHUNK] for s in sums], axis=0)
        placed = None
        for step in range(3):
            rounded = value.astype(jnp.bfloat16)
            term = lax.dot_general(chosen, rounded, (((1,), (1,)), ((), ())), preferred_element_type=jnp.float32)
            placed = term if placed is None else placed + term
            value = value - rounded.astype(jnp.float32)
        out[part] = placed

    for j in range(CHUNKS):
        for d in range(highs):
            pair_copy(d, j).wait_send()
        for d in range(1, highs):
            far_copy(d, j).wait_send()
        strip_copy(j).wait_send()
        for d in range(1, zs):
            slot_copy(d, j).wait_send()


def solution(mesh):
    cols, facs = mesh.shape["col"], mesh.shape["fac"]
    highs, zs = cols // 2, facs // 2

    def on_device(facets, row_taper, column_taper, column_place, row_offset, column_offset, slot_subgrid):
        rows, width = facets.shape[1], facets.shape[2]
        bf16, f32 = jnp.bfloat16, jnp.float32
        lanes = zs * STRIP
        part = (CHUNKS, 2 * CHUNK, width)
        slot = (CHUNKS, 2 * CHUNK, STRIP)
        far = max(highs - 1, 1)
        sem = pltpu.SemaphoreType.DMA
        smem = pl.BlockSpec(memory_space=pltpu.SMEM)
        vmem = pl.BlockSpec(memory_space=pltpu.VMEM)
        grid = pl.pallas_call(
            functools.partial(kernel, cols, facs),
            out_shape=jax.ShapeDtypeStruct((2, SUBGRID, STRIP), f32),
            in_specs=[smem] * 4 + [vmem] * 2 + [pl.BlockSpec(memory_space=pl.ANY)],
            out_specs=vmem,
            scratch_shapes=[
                pltpu.VMEM((2, rows, width), bf16),
                pltpu.VMEM((STRIP // FINE, rows), f32), pltpu.VMEM((STRIP // FINE, rows), f32),
                pltpu.VMEM((FINE, rows), f32), pltpu.VMEM((FINE, rows), f32),
                pltpu.VMEM((cols, 2 * STRIP, rows), bf16),
                pltpu.VMEM((2 * width, lanes), bf16), pltpu.VMEM((2 * width, lanes), bf16),
                pltpu.VMEM((highs, *part), bf16), pltpu.VMEM((highs, *part), bf16),
                pltpu.VMEM((far, *part), f32),
                pltpu.VMEM((far, *part), bf16), pltpu.VMEM((far, *part), bf16),
                pltpu.VMEM(part, f32),
                pltpu.VMEM(part, bf16), pltpu.VMEM(part, bf16),
                pltpu.VMEM((CHUNKS, 2 * CHUNK, lanes), f32),
                pltpu.VMEM(slot, f32),
                pltpu.VMEM((zs - 1, *slot), bf16), pltpu.VMEM((zs - 1, *slot), bf16),
                sem((2,)),
                sem((highs, CHUNKS)), sem((highs, CHUNKS)),
                sem((far, CHUNKS)), sem((far, CHUNKS)),
                sem((CHUNKS,)), sem((CHUNKS,)),
                sem((zs - 1, CHUNKS)), sem((zs - 1, CHUNKS)),
            ],
            compiler_params=pltpu.CompilerParams(
                collective_id=0, has_side_effects=True, vmem_limit_bytes=48 * 1024 * 1024),
        )(row_offset, column_offset, slot_subgrid, column_place,
          row_taper.reshape(1, -1), column_taper.reshape(1, -1), facets)
        return grid.reshape(1, 1, 2, SUBGRID, STRIP)

    in_specs = (P(None, "col", "fac"), P("col"), P(), P(), P(), P(), P())
    out_specs = P("col", "fac", None, None, None)
    return jax.shard_map(on_device, mesh=mesh, in_specs=in_specs, out_specs=out_specs, check_vma=False)
```

time: 135 us -> 31.6 us (0.23)
  other arithmetic: 57.1 us -> 0 us
  waiting for transfers between devices: 48.2 us -> 0 us
  Pallas kernels: 0 us -> 24.9 us
  between operations: 14.2 us -> 0.67 us
  starting transfers between devices: 5.49 us -> 0 us
  matrix products: 4.02 us -> 0 us
    scatter-add x1 -> x0, other arithmetic: 32.8 us -> none  [on_device(): jnp.zeros((2, SUBGRID, STRIP), jnp.float32).at[:, targets, :].add(merged)]
    all_to_all x1 -> x0, waiting for transfers between devices: 24.9 us -> none  [on_device(): lax.all_to_all(contribution, 'fac', split_axis=1, concat_axis=1, tiled=True)]
    pallas_call x0 -> x1, Pallas kernels: none -> 24.9 us  [on_device(): pl.pallas_call(functools.partial(kernel, cols, facs), out_shape=jax.Shape...]
    reduce_scatter x1 -> x0, waiting for transfers between devices: 23.3 us -> none  [on_device(): lax.psum_scatter(jnp.concatenate([real_out, imag_out], axis=1), 'col', sc...]
    another operation x5 -> x0, other arithmetic: 19.7 us -> none
    all_to_all x1 -> x0, starting transfers between devices: 5.49 us -> none  [on_device(): lax.all_to_all(contribution, 'fac', split_axis=1, concat_axis=1, tiled=True)]
    dot_general x4 -> x0, matrix products: 4.02 us -> none  [the longest x1 1.31 us: complex_rows(): jnp.dot(stacked, real_part, preferred_element_type=jnp.float32)]
    unnamed x8 -> x13, local copies, waits for them, and re-layouts: 2.04 us -> 5.77 us
  transfers between devices with their start and end apart: 2 -> 0, of which waited for: 2 -> 0; matrix products, arithmetic and copies ran while one was open for 8% -> 0% of each run, Pallas kernels for 0% -> 0%
where the time goes in v1:
time: 31.6 us; the launch traced here: 31.3 us
  Pallas kernels  24.9 us (79%)
  local copies, waits for them, and re-layouts  5.77 us (18%)
  between operations  0.67 us (2%)
    pallas_call x1, Pallas kernels, on_device(): pl.pallas_call(functools.partial(kernel, cols, facs), out_shape=jax.Shape...  24.9 us
    unnamed x13, local copies, waits for them, and re-layouts  5.77 us

profile of v1, /device:TPU:0, one launch (start us, length us, event | category | flops | bytes accessed | tf_op | source)
XLA Modules:
  0.0 31.3 jit_solution(2542866397123700945)
XLA Ops:
  0.7 0.0 copy-start
  0.7 1.6 %copy-done = bf16[2,1024,512]{2,1,0:T(8,128)(2,1)S(1)} copy-done((bf16[2,1024,512]{2,1,0:T(8,128)(2,1)S(1)}, bf16[2,1024,512]{2,1,0:T(8,128)(2,1)}, u32[]{:S(2)}) %copy-start) | copy-done | bytes 2097176
  2.2 0.0 copy-start.1
  2.2 0.7 %copy-done.1 = f32[4096]{0:T(1024)S(1)} copy-done((f32[4096]{0:T(1024)S(1)}, f32[4096]{0:T(1024)}, u32[]{:S(2)}) %copy-start.1) | copy-done | bytes 16408
  3.0 0.0 copy-start.2
  3.0 0.7 %copy-done.2 = f32[1024]{0:T(1024)S(1)} copy-done((f32[1024]{0:T(1024)S(1)}, f32[1024]{0:T(1024)}, u32[]{:S(2)}) %copy-start.2) | copy-done | bytes 4120
  3.6 0.0 copy-start.3
  3.7 0.7 %copy-done.3 = s32[4,8]{1,0:T(4,128)S(1)} copy-done((s32[4,8]{1,0:T(4,128)S(1)}, s32[4,8]{1,0:T(4,128)}, u32[]{:S(2)}) %copy-start.3) | copy-done | bytes 152
  4.3 0.0 copy-start.4
  4.3 0.7 %copy-done.4 = s32[4]{0:T(128)S(1)} copy-done((s32[4]{0:T(128)S(1)}, s32[4]{0:T(128)}, u32[]{:S(2)}) %copy-start.4) | copy-done | bytes 40
  5.0 0.0 copy-start.5
  5.0 0.7 %copy-done.5 = s32[8]{0:T(128)S(1)} copy-done((s32[8]{0:T(128)S(1)}, s32[8]{0:T(128)}, u32[]{:S(2)}) %copy-start.5) | copy-done | bytes 56
  5.6 24.9 %shard_map.73 = f32[2,512,128]{2,1,0:T(8,128)S(1)} custom-call(s32[4]{0:T(128)S(1)} %copy-done.4, s32[8]{0:T(128)S(1)} %copy-done.5, s32[4,8]{1,0:T(4,128)S(1)} %copy-done.3, s32[1]{0:T(128)S(6)} %copy.9.column_place, f32[1,1024]{1,0:T(1,128)S(1)} %bitcast.5, f32[1,4096]{1,0:T(1,128)S(1)} %bitcast.4, bf16[2,1024,512]{2,1,0:T(8,128)(2,1)S(1)} %copy-done), custom_call_target="tpu_custom_call" | custom-call | tf_op jit(solution)/shard_map/pallas_call | solution.py:241
  30.5 0.8 %copy.10 = f32[1,1,2,512,128]{4,3,2,1,0:T(8,128)} copy(f32[1,1,2,512,128]{4,3,2,1,0:T(8,128)S(1)} %bitcast.3) | data formatting | bytes 1048576
Async XLA Ops:
  0.7 1.6 %copy-start = (bf16[2,1024,512]{2,1,0:T(8,128)(2,1)S(1)}, bf16[2,1024,512]{2,1,0:T(8,128)(2,1)}, u32[]{:S(2)}) copy-start(bf16[2,1024,512]{2,1,0:T(8,128)(2,1)} %facets.1) | copy-start | bytes 6291460
  2.2 0.7 %copy-start.1 = (f32[4096]{0:T(1024)S(1)}, f32[4096]{0:T(1024)}, u32[]{:S(2)}) copy-start(f32[4096]{0:T(1024)} %param.9) | copy-start | bytes 49156
  3.0 0.7 %copy-start.2 = (f32[1024]{0:T(1024)S(1)}, f32[1024]{0:T(1024)}, u32[]{:S(2)}) copy-start(f32[1024]{0:T(1024)} %param.8) | copy-start | bytes 12292
  3.6 0.7 %copy-start.3 = (s32[4,8]{1,0:T(4,128)S(1)}, s32[4,8]{1,0:T(4,128)}, u32[]{:S(2)}) copy-start(s32[4,8]{1,0:T(4,128)} %slot_subgrid.1) | copy-start | bytes 388
  4.3 0.7 %copy-start.4 = (s32[4]{0:T(128)S(1)}, s32[4]{0:T(128)}, u32[]{:S(2)}) copy-start(s32[4]{0:T(128)} %row_offset.1) | copy-start | bytes 52
  5.0 0.7 %copy-start.5 = (s32[8]{0:T(128)S(1)}, s32[8]{0:T(128)}, u32[]{:S(2)}) copy-start(s32[8]{0:T(128)} %column_offset.1) | copy-start | bytes 100

commit v2 on v1

--- a/solution.py
+++ b/solution.py
@@ -13,6 +13,7 @@
 SUBGRID = 512
 FINE = 16
 CHUNKS = 4
+LAG = 2
 CHUNK = STRIP // CHUNKS
 MESH = pl.DeviceIdType.MESH
 
@@ -39,12 +40,12 @@
 
 def kernel(
     cols, facs,
-    row_offset, column_offset, slot_subgrid, column_place, row_taper, column_taper, facets,
+    row_offset_in, column_offset_in, slot_subgrid_in, row_taper_in, column_taper_in, facets,
     out,
-    held, coarse_r, coarse_i, fine_r, fine_i, encode, decode_r, decode_i,
+    row_offset, column_offset, slot_subgrid, row_taper, column_gain, held, coarse_r, coarse_i, fine_r, fine_i, steep_r, steep_i, encode, decode_r, decode_i,
     pair_out, pair_in, far_part, far_out, far_in, own_part, strip, strip_in,
     half, mine, slots_out, slots_in,
-    held_sem, pair_send, pair_recv, far_send, far_recv, strip_send, strip_recv, slot_send, slot_recv,
+    zeros, placed, out_sem, small_sem, held_sem, pair_send, pair_recv, far_send, far_recv, strip_send, strip_recv, slot_send, slot_recv,
 ):
     col = lax.axis_index("col")
     fac = lax.axis_index("fac")
@@ -58,16 +59,25 @@
     strip_id = (col, fac_hi * 2 + 1 - fac_lo)
     slot_ids = [(col, (fac_hi + d) % zs * 2 + fac_lo) for d in range(1, zs)]
     peers = [pair_id, *far_ids, strip_id, *slot_ids]
+    own_columns = pl.ds(pl.multiple_of(fac * width, width), width)
+    small = [
+        pltpu.make_async_copy(source, target, small_sem.at[n])
+        for n, (source, target) in enumerate((
+            (row_offset_in, row_offset), (column_offset_in, column_offset), (slot_subgrid_in, slot_subgrid),
+            (row_taper_in, row_taper),
+            (column_taper_in.at[:, own_columns], column_gain)))]
+    loads = [pltpu.make_async_copy(facets.at[p], held.at[p], held_sem.at[p]) for p in range(2)]
+    for load in (*small, *loads):
+        load.start()
     barrier = pltpu.get_barrier_semaphore()
     for peer in peers:
         pl.semaphore_signal(barrier, inc=1, device_id=peer, device_id_type=MESH)
-    loads = [pltpu.make_async_copy(facets.at[p], held.at[p], held_sem.at[p]) for p in range(2)]
-    for load in loads:
-        load.start()
 
     steps = STRIP // FINE
     position = col * rows + iota((1, rows), 1)
     fine_r[...], fine_i[...] = unit_phase(iota((FINE, rows), 0) * position)
+    for load in small:
+        load.wait()
     gain = row_taper[...] * (1.0 / math.sqrt(FACET))
 
     def encode_group(index, group):
@@ -118,30 +128,38 @@
             src_ref=slots_out.at[d - 1, j], dst_ref=slots_in.at[d - 1, j], send_sem=slot_send.at[d - 1, j],
             recv_sem=slot_recv.at[d - 1, j], device_id=slot_ids[d - 1], device_id_type=MESH)
 
-    order = [*range(1, highs), 0]
-    for d in order:
+    zeros[...] = jnp.zeros_like(zeros)
+    blanks = [
+        pltpu.make_async_copy(
+            zeros, out.at[:, pl.ds(n * SUBGRID + STRIP, SUBGRID - STRIP), :], out_sem.at[0, n]) for n in range(2)]
+
+    def groups(d):
         high = (col_hi + d) % highs * 2
         encode_group(2 * d, high + 1 - core)
         encode_group(2 * d + 1, high + core)
 
+    for d in range(1, highs):
+        groups(d)
     for load in loads:
         load.wait()
+    for d in range(1, highs):
+        chunked(pair_out.at[d], *product(2 * d))
+        chunked(far_part.at[d - 1], *product(2 * d + 1))
     pl.semaphore_wait(barrier, len(peers))
-
-    def to_pair(d):
-        chunked(pair_out.at[d], *product(2 * d))
+    for d in range(1, highs):
         for j in range(CHUNKS):
             pair_copy(d, j).start()
-
-    for d in range(1, highs):
-        to_pair(d)
-        chunked(far_part.at[d - 1], *product(2 * d + 1))
-    to_pair(0)
+    groups(0)
+    chunked(pair_out.at[0], *product(0))
+    for j in range(CHUNKS):
+        pair_copy(0, j).start()
     for d in range(1, highs):
         for j in range(CHUNKS):
             pair_copy(d, j).wait_recv()
             far_out[d - 1, j] = (far_part[d - 1, j] + pair_in[d, j].astype(jnp.float32)).astype(jnp.bfloat16)
             far_copy(d, j).start()
+    for blank in blanks:
+        blank.start()
     chunked(own_part, *product(1))
 
     lanes = zs * STRIP
@@ -155,17 +173,16 @@
     fine_real, fine_imag = fine_real * (1.0 / math.sqrt(FACET)), fine_imag * (1.0 / math.sqrt(FACET))
     for part, block in enumerate((fac, fac_hi * 2 + 1 - fac_lo)):
         base = part * width
-
-        def row(i, carry, base=base, block=block):
-            ar, ai = unit_phase((block * width + i * FINE) * frequency)
+        steep_r[...], steep_i[...] = unit_phase((block * width + FINE * iota((coarse_n, lanes), 0)) * frequency)
+
+        def row(i, carry, base=base):
+            ar, ai = steep_r[pl.ds(i, 1), :], steep_i[pl.ds(i, 1), :]
             at = pl.multiple_of(base + i * FINE, FINE)
             decode_r[pl.ds(at, FINE), :] = (ar * fine_real - ai * fine_imag).astype(jnp.bfloat16)
             decode_i[pl.ds(at, FINE), :] = (ar * fine_imag + ai * fine_real).astype(jnp.bfloat16)
             return carry
 
         lax.fori_loop(0, coarse_n, row, 0)
-
-    column_gain = column_taper[:, pl.ds(pl.multiple_of(fac * width, width), width)]
 
     def decoded(block, part):
         span = slice(part * width, (part + 1) * width)
@@ -188,15 +205,14 @@
         for d in range(1, highs):
             far_copy(d, j).wait_recv()
             total = total + far_in[d - 1, j].astype(jnp.float32)
-        strip[j] = (total * column_gain).astype(jnp.bfloat16)
+        strip[j] = (total * column_gain[...]).astype(jnp.bfloat16)
         strip_copy(j).start()
         half[j] = decoded(strip[j], 0)
-        if j:
-            finish(j - 1)
-    finish(CHUNKS - 1)
-
-    place = (iota((SUBGRID, STRIP), 0) - column_place[0]) & (SUBGRID - 1)
-    chosen = (place == iota((SUBGRID, STRIP), 1)).astype(jnp.bfloat16)
+        if j >= LAG:
+            finish(j - LAG)
+    for j in range(CHUNKS - LAG, CHUNKS):
+        finish(j)
+
     sums = []
     for j in range(CHUNKS):
         total = mine[j]
@@ -206,14 +222,12 @@
         sums.append(total)
     for part in range(2):
         value = jnp.concatenate([s[part * CHUNK:(part + 1) * CHUNK] for s in sums], axis=0)
-        placed = None
-        for step in range(3):
-            rounded = value.astype(jnp.bfloat16)
-            term = lax.dot_general(chosen, rounded, (((1,), (1,)), ((), ())), preferred_element_type=jnp.float32)
-            placed = term if placed is None else placed + term
-            value = value - rounded.astype(jnp.float32)
-        out[part] = placed
-
+        placed[part] = value.T
+
+    puts = [
+        pltpu.make_async_copy(placed, out.at[:, pl.ds(n * SUBGRID, STRIP), :], out_sem.at[1, n]) for n in range(2)]
+    for put in puts:
+        put.start()
     for j in range(CHUNKS):
         for d in range(highs):
             pair_copy(d, j).wait_send()
@@ -222,6 +236,8 @@
         strip_copy(j).wait_send()
         for d in range(1, zs):
             slot_copy(d, j).wait_send()
+    for put in (*blanks, *puts):
+        put.wait()
 
 
 def solution(mesh):
@@ -236,17 +252,19 @@
         slot = (CHUNKS, 2 * CHUNK, STRIP)
         far = max(highs - 1, 1)
         sem = pltpu.SemaphoreType.DMA
-        smem = pl.BlockSpec(memory_space=pltpu.SMEM)
-        vmem = pl.BlockSpec(memory_space=pltpu.VMEM)
         grid = pl.pallas_call(
             functools.partial(kernel, cols, facs),
-            out_shape=jax.ShapeDtypeStruct((2, SUBGRID, STRIP), f32),
-            in_specs=[smem] * 4 + [vmem] * 2 + [pl.BlockSpec(memory_space=pl.ANY)],
-            out_specs=vmem,
+            out_shape=jax.ShapeDtypeStruct((2, 2 * SUBGRID, STRIP), f32),
+            in_specs=[pl.BlockSpec(memory_space=pltpu.HBM)] * 6,
+            out_specs=pl.BlockSpec(memory_space=pl.ANY),
             scratch_shapes=[
+                pltpu.SMEM(row_offset.shape, jnp.int32), pltpu.SMEM(column_offset.shape, jnp.int32),
+                pltpu.SMEM(slot_subgrid.shape, jnp.int32),
+                pltpu.VMEM((1, rows), f32), pltpu.VMEM((1, width), f32),
                 pltpu.VMEM((2, rows, width), bf16),
                 pltpu.VMEM((STRIP // FINE, rows), f32), pltpu.VMEM((STRIP // FINE, rows), f32),
                 pltpu.VMEM((FINE, rows), f32), pltpu.VMEM((FINE, rows), f32),
+                pltpu.VMEM((width // FINE, lanes), f32), pltpu.VMEM((width // FINE, lanes), f32),
                 pltpu.VMEM((cols, 2 * STRIP, rows), bf16),
                 pltpu.VMEM((2 * width, lanes), bf16), pltpu.VMEM((2 * width, lanes), bf16),
                 pltpu.VMEM((highs, *part), bf16), pltpu.VMEM((highs, *part), bf16),
@@ -257,16 +275,18 @@
                 pltpu.VMEM((CHUNKS, 2 * CHUNK, lanes), f32),
                 pltpu.VMEM(slot, f32),
                 pltpu.VMEM((zs - 1, *slot), bf16), pltpu.VMEM((zs - 1, *slot), bf16),
-                sem((2,)),
+                pltpu.VMEM((2, SUBGRID - STRIP, STRIP), f32), pltpu.VMEM((2, STRIP, STRIP), f32), sem((2, 2)),
+                sem((5,)), sem((2,)),
                 sem((highs, CHUNKS)), sem((highs, CHUNKS)),
                 sem((far, CHUNKS)), sem((far, CHUNKS)),
                 sem((CHUNKS,)), sem((CHUNKS,)),
                 sem((zs - 1, CHUNKS)), sem((zs - 1, CHUNKS)),
             ],
             compiler_params=pltpu.CompilerParams(
-                collective_id=0, has_side_effects=True, vmem_limit_bytes=48 * 1024 * 1024),
-        )(row_offset, column_offset, slot_subgrid, column_place,
+                collective_id=0, has_side_effects=True, vmem_limit_bytes=67_043_328),
+        )(row_offset, column_offset, slot_subgrid,
           row_taper.reshape(1, -1), column_taper.reshape(1, -1), facets)
+        grid = lax.dynamic_slice_in_dim(grid, SUBGRID - column_place[0], SUBGRID, axis=1)
         return grid.reshape(1, 1, 2, SUBGRID, STRIP)
 
     in_specs = (P(None, "col", "fac"), P("col"), P(), P(), P(), P(), P())

time: 31.6 us -> 27.5 us (0.87)
  local copies, waits for them, and re-layouts: 5.77 us -> 1.9 us
    unnamed x13 -> x0, local copies, waits for them, and re-layouts: 5.77 us -> none
    reshape x0 -> x1, local copies, waits for them, and re-layouts: none -> 1.9 us  [on_device(): return grid.reshape(1, 1, 2, SUBGRID, STRIP)]
where the time goes in v2:
time: 27.5 us; the launch traced here: 27.3 us
  Pallas kernels  24.7 us (90%)
  local copies, waits for them, and re-layouts  1.9 us (7%)
  between operations  0.67 us (2%)
    pallas_call x1, Pallas kernels, on_device(): pl.pallas_call(functools.partial(kernel, cols, facs), out_shape=jax.Shape...  24.7 us
    reshape x1, local copies, waits for them, and re-layouts, on_device(): return grid.reshape(1, 1, 2, SUBGRID, STRIP)  1.9 us

profile of v2, /device:TPU:0, one launch (start us, length us, event | category | flops | bytes accessed | tf_op | source)
XLA Modules:
  0.0 27.3 jit_solution(152089593585256645)
XLA Ops:
  0.7 24.7 %shard_map.73 = f32[2,1024,128]{2,1,0:T(8,128)} custom-call(s32[4]{0:T(128)} %row_offset_in.1, s32[8]{0:T(128)} %column_offset_in.1, s32[4,8]{1,0:T(4,128)} %slot_subgrid_in.1, f32[1,1024]{1,0:T(1,128)} %bitcast.7, f32[1,4096]{1,0:T(1,128)} %bitcast.6, bf16[2,1024,512]{2,1,0:T(8,128)(2,1)} %facets.1), custom_call_target="tpu_custom_call" | custom-call | tf_op jit(solution)/shard_map/pallas_call | solution.py:255
  25.4 1.9 %dynamic-slice_bitcast_fusion = f32[1,1,2,512,128]{4,3,2,1,0:T(8,128)} fusion(f32[2,1024,128]{2,1,0:T(8,128)} %shard_map.73, s32[]{:T(128)S(6)} %select_n.3), kind=kLoop, calls=%fused_computation | loop fusion | bytes 1048580 | tf_op jit(solution)/shard_map/reshape | solution.py:290

commit v3 on v2

--- a/solution.py
+++ b/solution.py
@@ -45,7 +45,7 @@
     row_offset, column_offset, slot_subgrid, row_taper, column_gain, held, coarse_r, coarse_i, fine_r, fine_i, steep_r, steep_i, encode, decode_r, decode_i,
     pair_out, pair_in, far_part, far_out, far_in, own_part, strip, strip_in,
     half, mine, slots_out, slots_in,
-    zeros, placed, out_sem, small_sem, held_sem, pair_send, pair_recv, far_send, far_recv, strip_send, strip_recv, slot_send, slot_recv,
+    small_sem, held_sem, pair_send, pair_recv, far_send, far_recv, strip_send, strip_recv, slot_send, slot_recv,
 ):
     col = lax.axis_index("col")
     fac = lax.axis_index("fac")
@@ -128,11 +128,6 @@
             src_ref=slots_out.at[d - 1, j], dst_ref=slots_in.at[d - 1, j], send_sem=slot_send.at[d - 1, j],
             recv_sem=slot_recv.at[d - 1, j], device_id=slot_ids[d - 1], device_id_type=MESH)
 
-    zeros[...] = jnp.zeros_like(zeros)
-    blanks = [
-        pltpu.make_async_copy(
-            zeros, out.at[:, pl.ds(n * SUBGRID + STRIP, SUBGRID - STRIP), :], out_sem.at[0, n]) for n in range(2)]
-
     def groups(d):
         high = (col_hi + d) % highs * 2
         encode_group(2 * d, high + 1 - core)
@@ -158,8 +153,6 @@
             pair_copy(d, j).wait_recv()
             far_out[d - 1, j] = (far_part[d - 1, j] + pair_in[d, j].astype(jnp.float32)).astype(jnp.bfloat16)
             far_copy(d, j).start()
-    for blank in blanks:
-        blank.start()
     chunked(own_part, *product(1))
 
     lanes = zs * STRIP
@@ -222,12 +215,8 @@
         sums.append(total)
     for part in range(2):
         value = jnp.concatenate([s[part * CHUNK:(part + 1) * CHUNK] for s in sums], axis=0)
-        placed[part] = value.T
-
-    puts = [
-        pltpu.make_async_copy(placed, out.at[:, pl.ds(n * SUBGRID, STRIP), :], out_sem.at[1, n]) for n in range(2)]
-    for put in puts:
-        put.start()
+        out[part] = value.T
+
     for j in range(CHUNKS):
         for d in range(highs):
             pair_copy(d, j).wait_send()
@@ -236,8 +225,12 @@
         strip_copy(j).wait_send()
         for d in range(1, zs):
             slot_copy(d, j).wait_send()
-    for put in (*blanks, *puts):
-        put.wait()
+
+
+def place_kernel(place, part, out):
+    blank = jnp.zeros((SUBGRID - STRIP, STRIP), jnp.float32)
+    for n in range(2):
+        out[n] = pltpu.roll(jnp.concatenate([part[n], blank], axis=0), place[0], 0)
 
 
 def solution(mesh):
@@ -254,9 +247,9 @@
         sem = pltpu.SemaphoreType.DMA
         grid = pl.pallas_call(
             functools.partial(kernel, cols, facs),
-            out_shape=jax.ShapeDtypeStruct((2, 2 * SUBGRID, STRIP), f32),
+            out_shape=jax.ShapeDtypeStruct((2, STRIP, STRIP), f32),
             in_specs=[pl.BlockSpec(memory_space=pltpu.HBM)] * 6,
-            out_specs=pl.BlockSpec(memory_space=pl.ANY),
+            out_specs=pl.BlockSpec(memory_space=pltpu.VMEM),
             scratch_shapes=[
                 pltpu.SMEM(row_offset.shape, jnp.int32), pltpu.SMEM(column_offset.shape, jnp.int32),
                 pltpu.SMEM(slot_subgrid.shape, jnp.int32),
@@ -275,7 +268,6 @@
                 pltpu.VMEM((CHUNKS, 2 * CHUNK, lanes), f32),
                 pltpu.VMEM(slot, f32),
                 pltpu.VMEM((zs - 1, *slot), bf16), pltpu.VMEM((zs - 1, *slot), bf16),
-                pltpu.VMEM((2, SUBGRID - STRIP, STRIP), f32), pltpu.VMEM((2, STRIP, STRIP), f32), sem((2, 2)),
                 sem((5,)), sem((2,)),
                 sem((highs, CHUNKS)), sem((highs, CHUNKS)),
                 sem((far, CHUNKS)), sem((far, CHUNKS)),
@@ -286,7 +278,12 @@
                 collective_id=0, has_side_effects=True, vmem_limit_bytes=67_043_328),
         )(row_offset, column_offset, slot_subgrid,
           row_taper.reshape(1, -1), column_taper.reshape(1, -1), facets)
-        grid = lax.dynamic_slice_in_dim(grid, SUBGRID - column_place[0], SUBGRID, axis=1)
+        grid = pl.pallas_call(
+            place_kernel,
+            out_shape=jax.ShapeDtypeStruct((2, SUBGRID, STRIP), f32),
+            in_specs=[pl.BlockSpec(memory_space=pltpu.SMEM), pl.BlockSpec(memory_space=pltpu.VMEM)],
+            out_specs=pl.BlockSpec(memory_space=pltpu.VMEM),
+        )(column_place, grid)
         return grid.reshape(1, 1, 2, SUBGRID, STRIP)
 
     in_specs = (P(None, "col", "fac"), P("col"), P(), P(), P(), P(), P())

time: 27.5 us -> 27.3 us (level)
  local copies, waits for them, and re-layouts: 1.9 us -> 0 us
  Pallas kernels: 24.7 us -> 26.5 us
    reshape x1 -> x0, local copies, waits for them, and re-layouts: 1.9 us -> none  [on_device(): return grid.reshape(1, 1, 2, SUBGRID, STRIP)]
    pallas_call x0 -> x1, Pallas kernels: none -> 1.78 us  [on_device(): pl.pallas_call(place_kernel, out_shape=jax.ShapeDtypeStruct((2, SUBGRID,...]
where the time goes in v3:
time: 27.3 us; the launch traced here: 27.1 us
  Pallas kernels  26.5 us (97%)
  between operations  0.66 us (2%)
    pallas_call x1, Pallas kernels, on_device(): pl.pallas_call(functools.partial(kernel, cols, facs), out_shape=jax.Shape...  24.7 us
    pallas_call x1, Pallas kernels, on_device(): pl.pallas_call(place_kernel, out_shape=jax.ShapeDtypeStruct((2, SUBGRID,...  1.78 us

profile of v3, /device:TPU:0, one launch (start us, length us, event | category | flops | bytes accessed | tf_op | source)
XLA Modules:
  0.0 27.1 jit_solution(13452593477009906048)
XLA Ops:
  0.7 24.7 %shard_map.73.part = f32[2,128,128]{2,1,0:T(8,128)} custom-call(s32[4]{0:T(128)} %row_offset_in.1, s32[8]{0:T(128)} %column_offset_in.1, s32[4,8]{1,0:T(4,128)} %slot_subgrid_in.1, f32[1,1024]{1,0:T(1,128)} %bitcast.4, f32[1,4096]{1,0:T(1,128)} %bitcast.3, bf16[2,1024,512]{2,1,0:T(8,128)(2,1)} %facets.1), custom_call_target="tpu_custom_call" | custom-call | tf_op jit(solution)/shard_map/pallas_call | solution.py:248
  25.3 1.8 %shard_map.74 = f32[2,512,128]{2,1,0:T(8,128)} custom-call(s32[1]{0:T(128)S(6)} %copy.8.place, f32[2,128,128]{2,1,0:T(8,128)} %shard_map.73.part), custom_call_target="tpu_custom_call" | custom-call | tf_op jit(solution)/shard_map/pallas_call | solution.py:281
